TPU v7x, 32 devices: a whole 2x2x4 slice. The times are simulated.
32 devices in a mesh: leaf: 2 (over core), blk: 4 (over y, x), col: 4 (over z).
Axes of the slice: x: 2, y: 2, z: 4, core: 2. Of those that a mesh axis runs over, the one named last changes fastest.
Arguments:
- front_sizes: int32 [2], replicated, may hold values from 1024 to 2048, as said below
- unit_rows: int32 [512], P('col'), may hold values from 0 to 4095, as said below
- target_rows: int32 [32, 512], P(None, 'col'), may hold values from 0 to 2047, as said below
- leaf_inverse: bfloat16 [4096, 2048], P(('leaf', 'blk')), may hold values from -0.125 to 0.125
- leaf_coupling: bfloat16 [256, 4096], P(None, ('leaf', 'blk')), may hold values from -0.59765625 to 0.59765625
- sep_factor: bfloat16 [256, 256], P(('leaf', 'blk'))
Outputs:
- entries: float32 [32, 512], P(('leaf', 'blk'), 'col')
Inputs may be any that keep to these rules, and one draw needn't show every extreme that they name: `front_sizes`: one leaf has exactly 2048 live rows. The offset of each unit (unit_rows mod 2048) is below the front size of its leaf. `target_rows`: each offset lies in the front of the leaf that holds the column's unit, padding rows included.
All inputs are finite; a program needn't handle non-finite values.
Results may differ from a plain program's by a relative error of at most 0.014.
Values sent between devices are 32-bit elements; how exact they have to be, the bound alone decides.
A program may use at most 64 MiB of HBM per device.

v0:
```python
import jax
import jax.numpy as jnp
from jax import lax
from jax.sharding import PartitionSpec as P


def from_partner(x, axis, stride):
    return lax.ppermute(x, axis, [(i, i ^ 1 << stride) for i in range(lax.axis_size(axis))])


def level_layout(level_count, unit):
    widths = [0] + [unit * 2 ** (level - 1) for level in range(1, level_count + 1)]
    starts = [0] * (level_count + 1)
    running = 0
    for level in range(1, level_count + 1):
        starts[level] = running
        running += widths[level]
    couplings = {}
    for source in range(1, level_count + 1):
        for ancestor in range(source + 1, level_count + 1):
            couplings[source, ancestor] = running
            running += widths[ancestor]
    return (widths, starts, couplings)


def per_device(front_sizes, unit_rows, target_rows, leaf_inverse, leaf_coupling, sep_factor):
    team_count = lax.axis_size("leaf")
    level_count = team_count.bit_length() - 1
    lane_count = lax.axis_size("blk")
    team = lax.axis_index("leaf")
    lane = lax.axis_index("blk")
    own_rows, leaf_width = leaf_inverse.shape
    sep_rows = sep_factor.shape[0]
    widths, starts, couplings = level_layout(level_count, sep_rows * lane_count * 2)
    contract = (((0,), (0,)), ((), ()))

    def block_total(amount, level):
        total = lax.psum(amount, "blk")
        for bit in range(level):
            total = total + from_partner(total, "leaf", bit)
        return total

    front = jnp.sum(jnp.where(jnp.arange(team_count) == team, front_sizes, 0))
    row_index = lane * own_rows + jnp.arange(own_rows)
    live = (row_index < front)[:, None]
    column_leaf = unit_rows // leaf_width
    onehot = (unit_rows[None, :] == team * leaf_width + jnp.arange(leaf_width)[:, None]).astype(
        jnp.bfloat16
    )
    leaf_y = jnp.where(
        live, jnp.dot(leaf_inverse, onehot, preferred_element_type=jnp.float32), 0.0
    ).astype(jnp.bfloat16)
    pushed = jnp.dot(leaf_coupling, leaf_y, preferred_element_type=jnp.float32)
    upward = [None] + [
        pushed[starts[level] : starts[level] + widths[level]] for level in range(1, level_count + 1)
    ]
    solved = [None] * (level_count + 1)
    for level in range(1, level_count + 1):
        total = block_total(upward[level], level)
        right = (-total).astype(jnp.bfloat16)
        inverse = sep_factor[:, starts[level] : starts[level] + widths[level]]
        solved[level] = jnp.dot(inverse, right, preferred_element_type=jnp.float32).astype(
            jnp.bfloat16
        )
        for ancestor in range(level + 1, level_count + 1):
            begin = couplings[level, ancestor]
            block = sep_factor[:, begin : begin + widths[ancestor]]
            upward[ancestor] = upward[ancestor] + lax.dot_general(
                block, solved[level], contract, preferred_element_type=jnp.float32
            )
    settled = [None] * (level_count + 1)
    for level in range(level_count, 0, -1):
        reduced = solved[level].astype(jnp.float32)
        for ancestor in range(level + 1, level_count + 1):
            begin = couplings[level, ancestor]
            block = sep_factor[:, begin : begin + widths[ancestor]]
            reduced = reduced - jnp.dot(
                block, settled[ancestor], preferred_element_type=jnp.float32
            )
        reduced = reduced.astype(jnp.bfloat16)
        inverse = sep_factor[:, starts[level] : starts[level] + widths[level]]
        portion = lax.dot_general(inverse, reduced, contract, preferred_element_type=jnp.float32)
        settled[level] = block_total(portion, level).astype(jnp.bfloat16)
    ancestors = jnp.concatenate(settled[1:], axis=0)
    leaf_z = (
        leaf_y.astype(jnp.float32)
        - lax.dot_general(leaf_coupling, ancestors, contract, preferred_element_type=jnp.float32)
    ).astype(jnp.bfloat16)
    terms = lax.dot_general(leaf_inverse, leaf_z, contract, preferred_element_type=jnp.float32)
    leaf_x = jnp.where(live, lax.psum_scatter(terms, "blk", scatter_dimension=0, tiled=True), 0.0)
    shifted = target_rows - lane * own_rows
    mine = (column_leaf == team)[None, :] & (shifted >= 0) & (shifted < own_rows)
    values = jnp.take_along_axis(leaf_x, jnp.clip(shifted, 0, own_rows - 1), axis=0)
    picks = jnp.where(mine, values, 0.0)
    return lax.psum_scatter(picks, ("leaf", "blk"), scatter_dimension=0, tiled=True)


def solution(mesh):
    placed = (
        P(),
        P("col"),
        P(None, "col"),
        P(("leaf", "blk"), None),
        P(None, ("leaf", "blk")),
        P(("leaf", "blk"), None),
    )
    return jax.shard_map(
        per_device, mesh=mesh, in_specs=placed, out_specs=P(("leaf", "blk"), "col"), check_vma=False
    )
```

profile of v0, /device:TPU:0, one launch (start us, length us, event | category | flops | bytes accessed | tf_op | source)
XLA Modules:
  0.0 201.9 jit_solution(13418508862043480203)
XLA Ops:
  6.6 1.4 fusion.7
  8.0 0.7 add_compare_fusion
  8.7 1.9 fusion.1
  10.6 0.9 convolution_bitcast_fusion.1
  11.5 0.0 all-reduce.4.cloned.1.call-update
  11.5 0.0 all-reduce.6.cloned.1.call-start
  11.6 45.0 %all-reduce.4.cloned.1.call-done = f32[256,128]{0,1:T(8,128)} async-done(((f32[256,128]{0,1:T(8,128)}), f32[256,128]{0,1:T(8,128)}) %all-reduce.4.cloned.1.call-update) | async-done | bytes 131088 | tf_op jit(solution)/shard_map/psum | solution.py:38
  56.6 1.6 collective-permute-done
  58.2 1.9 convolution_bitcast_fusion.2
  60.1 0.0 all-reduce.6.cloned.1.call-update
  60.1 0.0 copy-start.5
  60.1 0.0 copy-start.4
  60.1 0.0 copy-start.2
  60.1 0.0 reduce-scatter.2.cloned.1.call-start
  60.2 42.3 %all-reduce.6.cloned.1.call-done = f32[256,128]{0,1:T(8,128)} async-done(((f32[256,128]{0,1:T(8,128)}), f32[256,128]{0,1:T(8,128)}) %all-reduce.6.cloned.1.call-update) | async-done | bytes 131088 | tf_op jit(solution)/shard_map/psum | solution.py:38
  102.5 1.6 collective-permute-done.1
  104.0 2.4 %convolution_bitcast_fusion = f32[2048,128]{0,1:T(8,128)} fusion(bf16[512,2048]{1,0:T(8,128)(2,1)S(1)} %copy-done, bf16[256,512]{1,0:T(8,128)(2,1)S(1)} %copy-done.1, bf16[128,512]{1,0:T(8,128)(2,1)S(1)} %fusion.1, f32[256,128]{0,1:T(8,128)} %all-reduce.6.cloned.1.call-done, f32[256,128]{0,1:T(8,128)S(1)} %collective-permute-done.1), kind=kOutput, calls=%fused_computation.1 | convolution fusion | flops 302252032 | bytes 3801088 | tf_op jit(solution)/shard_map/dot_general | solution.py:89
  106.5 0.0 reduce-scatter.2.cloned.1.call-update
  106.5 0.6 dynamic-slice
  107.8 26.8 %reduce-scatter.2.cloned.1.call-done = f32[512,128]{0,1:T(8,128)} async-done(((f32[2048,128]{0,1:T(8,128)}), f32[512,128]{0,1:T(8,128)}) %reduce-scatter.2.cloned.1.call-update) | async-done | bytes 262160 | tf_op jit(solution)/shard_map/reduce_scatter | solution.py:90
  134.6 1.0 broadcast_select_fusion
  135.6 32.8 %gather_fusion = f32[4096]{0:T(1024)S(1)} fusion(f32[512,128]{0,1:T(8,128)S(1)} %broadcast_select_fusion, s32[4096]{0:T(1024)S(1)} %fusion.6), kind=kCustom, calls=%fused_computation | custom fusion | bytes 65536 | tf_op jit(solution)/shard_map/jit(take_along_axis)/gather | solution.py:93
  168.4 26.5 %all-reduce = f32[32,128]{1,0:T(8,128)S(1)} all-reduce(f32[32,128]{1,0:T(8,128)S(1)} %fusion.5), channel_id=3, replica_groups=mesh['leaf'=2,'blk'=4,'col'=4] {'leaf','blk'}, use_global_device_ids=true, to_apply=%region_4.5.clone | all-reduce | flops 4096 | bytes 32768
  194.8 0.6 constant_dynamic-slice_fusion
  (16 shorter events, 0.1 us)
Async XLA Ops:
  6.5 2.1 %copy-start = (bf16[512,2048]{1,0:T(8,128)(2,1)S(1)}, bf16[512,2048]{1,0:T(8,128)(2,1)}, u32[]{:S(2)}) copy-start(bf16[512,2048]{1,0:T(8,128)(2,1)} %param.9) | copy-start | bytes 6291460
  6.5 4.1 %copy-start.1 = (bf16[256,512]{1,0:T(8,128)(2,1)S(1)}, bf16[256,512]{1,0:T(8,128)(2,1)}, u32[]{:S(2)}) copy-start(bf16[256,512]{1,0:T(8,128)(2,1)} %param.10) | copy-start | bytes 786436
  6.5 51.6 %copy-start.3 = (bf16[32,256]{1,0:T(8,128)(2,1)S(1)}, bf16[32,256]{1,0:T(8,128)(2,1)}, u32[]{:S(2)}) copy-start(bf16[32,256]{1,0:T(8,128)(2,1)} %param.11) | copy-start | bytes 49156
  6.5 50.1 %all-reduce.4.cloned.1.call-start = ((), (), s32[]{:S(2)}) async-start(), calls=%async_computation.1 | async-start | bytes 262144 | tf_op jit(solution)/shard_map/psum | solution.py:38
  11.5 91.0 %all-reduce.6.cloned.1.call-start = ((), (), s32[]{:S(2)}) async-start(), calls=%async_computation.2 | async-start | bytes 262144 | tf_op jit(solution)/shard_map/psum | solution.py:38
  56.6 1.6 collective-permute-start
  60.1 46.4 %copy-start.5 = (u32[32]{0:T(128)S(1)}, u32[32]{0:T(128)}, u32[]{:S(2)}) copy-start(u32[32]{0:T(128)} %constant.65) | copy-start | bytes 388
  60.1 47.6 %copy-start.4 = (s32[128]{0:T(128)S(1)}, s32[128]{0:T(128)}, u32[]{:S(2)}) copy-start(s32[128]{0:T(128)} %param.7) | copy-start | bytes 1540
  60.1 47.7 %copy-start.2 = (s32[32,128]{1,0:T(8,128)S(1)}, s32[32,128]{1,0:T(8,128)}, u32[]{:S(2)}) copy-start(s32[32,128]{1,0:T(8,128)} %param.8) | copy-start | bytes 49156
  60.1 74.4 %reduce-scatter.2.cloned.1.call-start = ((), (), s32[]{:S(2)}) async-start(), calls=%async_computation.3 | async-start | bytes 1310720 | tf_op jit(solution)/shard_map/reduce_scatter | solution.py:90
  102.5 1.6 collective-permute-start.1
Sparse Core Ops, SparseCore 0:
  11.6 44.9 all-reduce.3
  60.2 42.2 all-reduce.5
  106.6 27.9 reduce-scatter.1
where the time goes:
time: 202 us
  waiting for transfers between devices  117 us (58%)
  local copies, waits for them, and re-layouts  34 us (17%)
  blocking collectives  26.5 us (13%)
  between operations  13.9 us (7%)
  matrix products  7.15 us (4%)
  other arithmetic  3.11 us (2%)
    psum x2, waiting for transfers between devices, block_total(): total = lax.psum(amount, 'blk')  87.3 us
    gather x1, local copies, waits for them, and re-layouts, per_device(): jnp.take_along_axis(leaf_x, jnp.clip(shifted, 0, own_rows - 1), axis=0)  32.8 us
    reduce_scatter x1, waiting for transfers between devices, per_device(): lax.psum_scatter(terms, 'blk', scatter_dimension=0, tiled=True)  26.8 us
    unnamed x1, blocking collectives  26.5 us
  transfers between devices with their start and end apart: 5, of which 5 were waited for; matrix products, arithmetic and copies ran while one was open for 0% of the time, Pallas kernels for 0%

commit v1 on v0

--- a/solution.py
+++ b/solution.py
@@ -1,7 +1,16 @@
+import functools
+
 import jax
 import jax.numpy as jnp
 from jax import lax
+from jax.experimental import pallas as pl
+from jax.experimental.pallas import tpu as pltpu
 from jax.sharding import PartitionSpec as P
+
+MESH = pl.DeviceIdType.MESH
+LANES = 128
+LOADS = 4
+CHUNKS = 2
 
 
 def from_partner(x, axis, stride):
@@ -23,7 +32,7 @@
     return (widths, starts, couplings)
 
 
-def per_device(front_sizes, unit_rows, target_rows, leaf_inverse, leaf_coupling, sep_factor):
+def many_levels(front_sizes, unit_rows, target_rows, leaf_inverse, leaf_coupling, sep_factor):
     team_count = lax.axis_size("leaf")
     level_count = team_count.bit_length() - 1
     lane_count = lax.axis_size("blk")
@@ -87,12 +96,276 @@
         - lax.dot_general(leaf_coupling, ancestors, contract, preferred_element_type=jnp.float32)
     ).astype(jnp.bfloat16)
     terms = lax.dot_general(leaf_inverse, leaf_z, contract, preferred_element_type=jnp.float32)
-    leaf_x = jnp.where(live, lax.psum_scatter(terms, "blk", scatter_dimension=0, tiled=True), 0.0)
-    shifted = target_rows - lane * own_rows
-    mine = (column_leaf == team)[None, :] & (shifted >= 0) & (shifted < own_rows)
-    values = jnp.take_along_axis(leaf_x, jnp.clip(shifted, 0, own_rows - 1), axis=0)
-    picks = jnp.where(mine, values, 0.0)
+    mine = (column_leaf == team)[None, :] & (target_rows < front)
+    picks = jnp.where(mine, jnp.take_along_axis(terms, target_rows, axis=0), 0.0)
     return lax.psum_scatter(picks, ("leaf", "blk"), scatter_dimension=0, tiled=True)
+
+
+def solve_kernel(
+    teams,
+    lanes,
+    front_hbm,
+    unit_hbm,
+    target_hbm,
+    inverse_hbm,
+    coupling_hbm,
+    sep_hbm,
+    out_ref,
+    front,
+    unit,
+    target,
+    inverse,
+    coupling,
+    sep,
+    leaf_y,
+    whole_sep,
+    part,
+    part_in,
+    half,
+    half_in,
+    picks,
+    picks_in,
+    load_sem,
+    sep_send,
+    sep_recv,
+    sum_send,
+    sum_recv,
+    pick_send,
+    pick_recv,
+):
+    team = lax.axis_index("leaf")
+    lane = lax.axis_index("blk")
+    place = team * lanes + lane
+    rows, width = inverse.shape
+    size = coupling.shape[0]
+    columns = unit.shape[1]
+    own_sep = sep.shape[0]
+    out_rows = out_ref.shape[0]
+    bits = lanes.bit_length() - 1
+    stride = rows // LOADS
+    f32, bf16 = jnp.float32, jnp.bfloat16
+
+    def device(other_team, other_lane):
+        return {"leaf": other_team, "blk": other_lane}
+
+    others = [(t, k) for t in range(teams) for k in range(lanes) if (t, k) != (0, 0)]
+
+    loads = [
+        pltpu.make_async_copy(front_hbm, front, load_sem.at[0]),
+        pltpu.make_async_copy(unit_hbm, unit, load_sem.at[1]),
+        pltpu.make_async_copy(sep_hbm, sep, load_sem.at[2]),
+    ]
+    blocks = [
+        pltpu.make_async_copy(
+            inverse_hbm.at[pl.ds(i * stride, stride)],
+            inverse.at[pl.ds(i * stride, stride)],
+            load_sem.at[5 + i],
+        )
+        for i in range(LOADS)
+    ]
+    later = [
+        pltpu.make_async_copy(coupling_hbm, coupling, load_sem.at[3]),
+        pltpu.make_async_copy(target_hbm, target, load_sem.at[4]),
+    ]
+    for copy in loads + blocks + later:
+        copy.start()
+
+    barrier = pltpu.get_barrier_semaphore()
+    for t, k in others:
+        pl.semaphore_signal(
+            barrier, inc=1, device_id=device(team ^ t, lane ^ k), device_id_type=MESH
+        )
+
+    for copy in loads:
+        copy.wait()
+    own = pl.ds(pl.multiple_of(place * own_sep, own_sep), own_sep)
+    whole_sep[own, :] = sep[...].astype(f32)
+    offset = unit[...] - team * width
+    onehot = (lax.broadcasted_iota(jnp.int32, (width, columns), 0) == offset).astype(f32).astype(bf16)
+
+    pl.semaphore_wait(barrier, len(others))
+
+    def sep_copy(slot, piece, other_team, other_lane):
+        block = pl.ds(pl.multiple_of(piece * own_sep, own_sep), own_sep)
+        return pltpu.make_async_remote_copy(
+            src_ref=whole_sep.at[block],
+            dst_ref=whole_sep.at[block],
+            send_sem=sep_send.at[slot],
+            recv_sem=sep_recv.at[slot],
+            device_id=device(other_team, other_lane),
+            device_id_type=MESH,
+        )
+
+    wide = [sep_copy(k, place, team, lane ^ k) for k in range(1, lanes)]
+    for copy in wide:
+        copy.start()
+    across = [sep_copy(lanes, place, team ^ 1, lane)]
+    across[0].start()
+
+    later[0].wait()
+    live_end = front[team] - lane * rows
+    pushed = None
+    for i in range(LOADS):
+        blocks[i].wait()
+        block = pl.ds(i * stride, stride)
+        values = jnp.dot(inverse[block, :], onehot, preferred_element_type=f32)
+        index = lax.broadcasted_iota(jnp.int32, (stride, columns), 0) + i * stride
+        values = jnp.where(index < live_end, values, 0.0)
+        leaf_y[block, :] = values
+        term = jnp.dot(coupling[:, block], values.astype(bf16), preferred_element_type=f32)
+        pushed = term if pushed is None else pushed + term
+    part[...] = pushed
+
+    chunk = size // (bits * CHUNKS)
+
+    def exchange(step, share, piece, source, target_ref):
+        slot = (step * bits + share) * CHUNKS + piece
+        block = pl.ds((share * CHUNKS + piece) * chunk, chunk)
+        return pltpu.make_async_remote_copy(
+            src_ref=source.at[block],
+            dst_ref=target_ref.at[block],
+            send_sem=sum_send.at[slot],
+            recv_sem=sum_recv.at[slot],
+            device_id=device(team, lane ^ (1 << (share + step) % bits)),
+            device_id_type=MESH,
+        )
+
+    order = [(share, piece) for piece in range(CHUNKS) for share in range(bits)]
+    sums = [part] + [half.at[i] for i in range(bits - 1)]
+    arrive = [part_in] + [half_in.at[i] for i in range(bits - 1)]
+    flights = [
+        {key: exchange(step, *key, sums[step], arrive[step]) for key in order}
+        for step in range(bits)
+    ]
+    for key in order:
+        flights[0][key].start()
+
+    for k in range(1, lanes):
+        wide[k - 1].wait_recv()
+        copy = sep_copy(lanes + k, team * lanes + (lane ^ k), team ^ 1, lane)
+        copy.start()
+        across.append(copy)
+    later[1].wait()
+    y_turned = leaf_y[...].T
+    count = target.shape[0]
+    padded = jnp.concatenate(
+        [target[...], jnp.zeros((LANES - count, columns), jnp.int32)], axis=0
+    )
+    wanted = padded.T
+    low = wanted % LANES
+    high = wanted // LANES
+
+    for step in range(1, bits):
+        for share, piece in order:
+            block = pl.ds((share * CHUNKS + piece) * chunk, chunk)
+            flights[step - 1][share, piece].wait_recv()
+            sums[step][block, :] = sums[step - 1][block, :] + arrive[step - 1][block, :]
+            flights[step][share, piece].start()
+
+    for copy in across:
+        copy.wait_recv()
+    matrix = whole_sep[...].astype(bf16)
+
+    for key in order:
+        flights[bits - 1][key].wait_recv()
+    right = (-(sums[bits - 1][...] + arrive[bits - 1][...])).astype(bf16)
+    sep_y = jnp.dot(matrix, right, preferred_element_type=f32)
+    sep_z = sep_y.T.astype(bf16)
+    sep_x = jnp.dot(sep_z, matrix, preferred_element_type=f32).astype(bf16)
+    leaf_z = (
+        y_turned.astype(bf16).astype(f32)
+        - jnp.dot(sep_x, coupling[...], preferred_element_type=f32)
+    ).astype(bf16)
+
+    found = jnp.zeros((columns, LANES), f32)
+    for i in range(width // LANES):
+        terms = jnp.dot(
+            leaf_z, inverse[:, i * LANES : (i + 1) * LANES], preferred_element_type=f32
+        )
+        here = jnp.take_along_axis(terms, low, axis=1)
+        found = jnp.where(high == i, here, found)
+    mine = (offset >= 0) & (offset < width) & (target[...] < front[team])
+    chosen = jnp.where(mine, found.T[:count], 0.0)
+    for i in range(teams * lanes):
+        picks[i] = chosen[i * out_rows : (i + 1) * out_rows]
+
+    gathers = []
+    for i, (t, k) in enumerate(others):
+        other = (team ^ t) * lanes + (lane ^ k)
+        gathers.append(
+            pltpu.make_async_remote_copy(
+                src_ref=picks.at[other],
+                dst_ref=picks_in.at[i],
+                send_sem=pick_send.at[i],
+                recv_sem=pick_recv.at[i],
+                device_id=device(team ^ t, lane ^ k),
+                device_id_type=MESH,
+            )
+        )
+    for copy in gathers:
+        copy.start()
+    total = picks[place]
+    for i, copy in enumerate(gathers):
+        copy.wait_recv()
+        total = total + picks_in[i]
+    out_ref[...] = total
+
+    for copy in wide + across + gathers:
+        copy.wait_send()
+    for flight in flights:
+        for key in order:
+            flight[key].wait_send()
+
+
+def one_level(front_sizes, unit_rows, target_rows, leaf_inverse, leaf_coupling, sep_factor):
+    teams = lax.axis_size("leaf")
+    lanes = lax.axis_size("blk")
+    rows, width = leaf_inverse.shape
+    size = leaf_coupling.shape[0]
+    columns = unit_rows.shape[0]
+    count = target_rows.shape[0]
+    group = teams * lanes
+    bits = lanes.bit_length() - 1
+    f32, bf16 = jnp.float32, jnp.bfloat16
+    anywhere = pl.BlockSpec(memory_space=pl.ANY)
+    dma = pltpu.SemaphoreType.DMA
+    return pl.pallas_call(
+        functools.partial(solve_kernel, teams, lanes),
+        out_shape=jax.ShapeDtypeStruct((count // group, columns), f32),
+        in_specs=[anywhere] * 6,
+        out_specs=pl.BlockSpec(memory_space=pltpu.VMEM),
+        scratch_shapes=[
+            pltpu.SMEM(front_sizes.shape, jnp.int32),
+            pltpu.VMEM((1, columns), jnp.int32),
+            pltpu.VMEM((count, columns), jnp.int32),
+            pltpu.VMEM((rows, width), bf16),
+            pltpu.VMEM((size, rows), bf16),
+            pltpu.VMEM(sep_factor.shape, bf16),
+            pltpu.VMEM((rows, columns), f32),
+            pltpu.VMEM((size, size), f32),
+            pltpu.VMEM((size, columns), f32),
+            pltpu.VMEM((size, columns), f32),
+            pltpu.VMEM((bits - 1, size, columns), f32),
+            pltpu.VMEM((bits - 1, size, columns), f32),
+            pltpu.VMEM((group, count // group, columns), f32),
+            pltpu.VMEM((group - 1, count // group, columns), f32),
+            dma((5 + LOADS,)),
+            dma((2 * lanes,)),
+            dma((2 * lanes,)),
+            dma((bits * bits * CHUNKS,)),
+            dma((bits * bits * CHUNKS,)),
+            dma((group - 1,)),
+            dma((group - 1,)),
+        ],
+        compiler_params=pltpu.CompilerParams(collective_id=0, has_side_effects=True),
+    )(
+        front_sizes,
+        unit_rows.reshape(1, columns),
+        target_rows,
+        leaf_inverse,
+        leaf_coupling,
+        sep_factor,
+    )
 
 
 def solution(mesh):
@@ -104,6 +377,7 @@
         P(None, ("leaf", "blk")),
         P(("leaf", "blk"), None),
     )
+    body = one_level if mesh.shape["leaf"] == 2 else many_levels
     return jax.shard_map(
-        per_device, mesh=mesh, in_specs=placed, out_specs=P(("leaf", "blk"), "col"), check_vma=False
-    )
+        body, mesh=mesh, in_specs=placed, out_specs=P(("leaf", "blk"), "col"), check_vma=False
+    )

time: 202 us -> 18.9 us (0.09)
  waiting for transfers between devices: 117 us -> 0 us
  local copies, waits for them, and re-layouts: 34 us -> 1.26 us
  blocking collectives: 26.5 us -> 0 us
  Pallas kernels: 0 us -> 17.4 us
  between operations: 13.9 us -> 0.01 us
  matrix products: 7.15 us -> 0 us
  other arithmetic: 3.11 us -> 0 us
    psum x2 -> x0, waiting for transfers between devices: 87.3 us -> none  [block_total(): total = lax.psum(amount, 'blk')]
    gather x1 -> x0, local copies, waits for them, and re-layouts: 32.8 us -> none  [per_device(): jnp.take_along_axis(leaf_x, jnp.clip(shifted, 0, own_rows - 1), axis=0)]
    reduce_scatter x1 -> x0, waiting for transfers between devices: 26.8 us -> none  [per_device(): lax.psum_scatter(terms, 'blk', scatter_dimension=0, tiled=True)]
    unnamed x1 -> x0, blocking collectives: 26.5 us -> none
    pallas_call x0 -> x1, Pallas kernels: none -> 17.4 us  [one_level(): pl.pallas_call(functools.partial(solve_kernel, teams, lanes), out_shape=j...]
    dot_general x4 -> x0, matrix products: 7.15 us -> none  [the longest x1 2.45 us: per_device(): lax.dot_general(leaf_inverse, leaf_z, contract, preferred_element_type=jn...]
    ppermute x2 -> x0, waiting for transfers between devices: 3.11 us -> none  [from_partner(): lax.ppermute(x, axis, [(i, i ^ 1 << stride) for i in range(lax.axis_size(...]
  transfers between devices with their start and end apart: 5 -> 0, of which waited for: 5 -> 0; matrix products, arithmetic and copies ran while one was open for 0% -> 0% of each run, Pallas kernels for 0% -> 0%
where the time goes in v1:
time: 18.9 us; the launch traced here: 18.7 us
  Pallas kernels  17.4 us (92%)
  local copies, waits for them, and re-layouts  1.26 us (7%)
    pallas_call x1, Pallas kernels, one_level(): pl.pallas_call(functools.partial(solve_kernel, teams, lanes), out_shape=j...  17.4 us
    unnamed x1, local copies, waits for them, and re-layouts  1.26 us

profile of v1, /device:TPU:0, one launch (start us, length us, event | category | flops | bytes accessed | tf_op | source)
XLA Modules:
  0.0 18.7 jit_solution(18313567426369145160)
XLA Ops:
  0.0 17.4 %shard_map.64 = f32[4,128]{1,0:T(4,128)} custom-call(s32[2]{0:T(128)} %front_hbm.1, s32[1,128]{1,0:T(1,128)} %bitcast.1, s32[32,128]{1,0:T(8,128)} %target_hbm.1, bf16[512,2048]{1,0:T(8,128)(2,1)} %inverse_hbm.1, bf16[256,512]{1,0:T(8,128)(2,1)} %coupling_hbm.1, bf16[32,256]{1,0:T(8,128)(2,1)} %sep_hbm.1), custom_call_target="tpu_custom_call" | custom-call | tf_op jit(solution)/shard_map/pallas_call | solution.py:332
  17.4 1.3 %copy.8 = f32[4,128]{1,0:T(4,128)} copy(f32[4,128]{1,0:T(4,128)} %shard_map.64) | data formatting | bytes 4096

commit v2 on v1

--- a/solution.py
+++ b/solution.py
@@ -11,6 +11,7 @@
 LANES = 128
 LOADS = 4
 CHUNKS = 2
+WIDE = 256
 
 
 def from_partner(x, axis, stride):
@@ -142,7 +143,7 @@
     own_sep = sep.shape[0]
     out_rows = out_ref.shape[0]
     bits = lanes.bit_length() - 1
-    stride = rows // LOADS
+    stride = width // LOADS
     f32, bf16 = jnp.float32, jnp.bfloat16
 
     def device(other_team, other_lane):
@@ -157,8 +158,8 @@
     ]
     blocks = [
         pltpu.make_async_copy(
-            inverse_hbm.at[pl.ds(i * stride, stride)],
-            inverse.at[pl.ds(i * stride, stride)],
+            inverse_hbm.at[:, pl.ds(i * stride, stride)],
+            inverse.at[:, pl.ds(i * stride, stride)],
             load_sem.at[5 + i],
         )
         for i in range(LOADS)
@@ -202,19 +203,18 @@
     across = [sep_copy(lanes, place, team ^ 1, lane)]
     across[0].start()
 
-    later[0].wait()
     live_end = front[team] - lane * rows
-    pushed = None
+    values = None
     for i in range(LOADS):
         blocks[i].wait()
-        block = pl.ds(i * stride, stride)
-        values = jnp.dot(inverse[block, :], onehot, preferred_element_type=f32)
-        index = lax.broadcasted_iota(jnp.int32, (stride, columns), 0) + i * stride
-        values = jnp.where(index < live_end, values, 0.0)
-        leaf_y[block, :] = values
-        term = jnp.dot(coupling[:, block], values.astype(bf16), preferred_element_type=f32)
-        pushed = term if pushed is None else pushed + term
-    part[...] = pushed
+        block = slice(i * stride, (i + 1) * stride)
+        term = jnp.dot(inverse[:, block], onehot[block], preferred_element_type=f32)
+        values = term if values is None else values + term
+    index = lax.broadcasted_iota(jnp.int32, (rows, columns), 0)
+    values = jnp.where(index < live_end, values, 0.0)
+    leaf_y[...] = values
+    later[0].wait()
+    part[...] = jnp.dot(coupling[...], values.astype(bf16), preferred_element_type=f32)
 
     chunk = size // (bits * CHUNKS)
 
@@ -278,12 +278,11 @@
     ).astype(bf16)
 
     found = jnp.zeros((columns, LANES), f32)
-    for i in range(width // LANES):
-        terms = jnp.dot(
-            leaf_z, inverse[:, i * LANES : (i + 1) * LANES], preferred_element_type=f32
-        )
-        here = jnp.take_along_axis(terms, low, axis=1)
-        found = jnp.where(high == i, here, found)
+    for start in range(0, width, WIDE):
+        terms = jnp.dot(leaf_z, inverse[:, start : start + WIDE], preferred_element_type=f32)
+        for i in range(WIDE // LANES):
+            here = jnp.take_along_axis(terms[:, i * LANES : (i + 1) * LANES], low, axis=1)
+            found = jnp.where(high == start // LANES + i, here, found)
     mine = (offset >= 0) & (offset < width) & (target[...] < front[team])
     chosen = jnp.where(mine, found.T[:count], 0.0)
     for i in range(teams * lanes):
@@ -331,7 +330,7 @@
     dma = pltpu.SemaphoreType.DMA
     return pl.pallas_call(
         functools.partial(solve_kernel, teams, lanes),
-        out_shape=jax.ShapeDtypeStruct((count // group, columns), f32),
+        out_shape=pltpu.VMEM((count // group, columns), f32),
         in_specs=[anywhere] * 6,
         out_specs=pl.BlockSpec(memory_space=pltpu.VMEM),
         scratch_shapes=[

time: 18.9 us -> 17.4 us (0.921)
  Pallas kernels: 17.4 us -> 16.7 us
  local copies, waits for them, and re-layouts: 1.26 us -> 0.58 us
    pallas_call x1, Pallas kernels: 17.4 us -> 16.7 us  [one_level(): pl.pallas_call(functools.partial(solve_kernel, teams, lanes), out_shape=p...]
    unnamed x1, local copies, waits for them, and re-layouts: 1.26 us -> 0.58 us
where the time goes in v2:
time: 17.4 us; the launch traced here: 17.3 us
  Pallas kernels  16.7 us (96%)
  local copies, waits for them, and re-layouts  0.58 us (3%)
    pallas_call x1, Pallas kernels, one_level(): pl.pallas_call(functools.partial(solve_kernel, teams, lanes), out_shape=p...  16.7 us
    unnamed x1, local copies, waits for them, and re-layouts  0.58 us

profile of v2, /device:TPU:0, one launch (start us, length us, event | category | flops | bytes accessed | tf_op | source)
XLA Modules:
  0.0 17.3 jit_solution(4914299830987266003)
XLA Ops:
  0.0 16.7 %shard_map.64 = f32[4,128]{1,0:T(4,128)S(1)} custom-call(s32[2]{0:T(128)} %front_hbm.1, s32[1,128]{1,0:T(1,128)} %bitcast.1, s32[32,128]{1,0:T(8,128)} %target_hbm.1, bf16[512,2048]{1,0:T(8,128)(2,1)} %inverse_hbm.1, bf16[256,512]{1,0:T(8,128)(2,1)} %coupling_hbm.1, bf16[32,256]{1,0:T(8,128)(2,1)} %sep_hbm.1), custom_call_target="tpu_custom_call" | custom-call | tf_op jit(solution)/shard_map/pallas_call | solution.py:331
  16.7 0.6 %copy.8 = f32[4,128]{1,0:T(4,128)} copy(f32[4,128]{1,0:T(4,128)S(1)} %shard_map.64) | data formatting | bytes 4096
